TPU v7x, 256 devices: a whole 4x4x8 slice. The times are simulated.
256 devices in a mesh: copy: 2 (over y_hi), dp: 8 (over x, core), fsdp: 16 (over y_lo, z).
Axes of the slice: x: 4, y: 4 (y_hi: 2, y_lo: 2; y = y_hi * 2 + y_lo), z: 8, core: 2. Of those that a mesh axis runs over, the one named last changes fastest.
Arguments:
- queries: bfloat16 [2, 128, 256, 2560], P('copy', ('dp', 'fsdp')), may hold values from -25 to 25
- keys: bfloat16 [2, 128, 256, 2560], P('copy', ('dp', 'fsdp')), may hold values from -25 to 25
- values: bfloat16 [2, 128, 256, 2560], P('copy', ('dp', 'fsdp')), may hold values from -6 to 6
- residual: bfloat16 [2, 128, 256, 2560], P('copy', ('dp', 'fsdp')), may hold values from -6 to 6
- event_ids: int32 [128, 256], P(('dp', 'fsdp')), may hold values from 0 to 1023
- lengths: int32 [128], replicated, may hold values from 8 to 256, as said below
- type_weight: float32 [1024], replicated, may hold values from 0.25 to 4
- w_out: bfloat16 [2, 2560, 2560], P('copy', 'fsdp'), may hold values from -0.125 to 0.125
- gain: float32 [2, 2560], P('copy'), may hold values from 0.5 to 1.5
Outputs:
- loss: float32 [2, 128], P('copy', ('dp', 'fsdp'))
- d_queries: bfloat16 [2, 128, 256, 2560], P('copy', ('dp', 'fsdp'))
- d_keys: bfloat16 [2, 128, 256, 2560], P('copy', ('dp', 'fsdp'))
- d_values: bfloat16 [2, 128, 256, 2560], P('copy', ('dp', 'fsdp'))
- d_wo: float32 [2, 2560, 2560], P('copy', 'fsdp')
Inputs may be any that keep to these rules, and one draw needn't show every extreme that they name: `lengths`: every history has at least 8 valid events and some history has all 256.
All inputs are finite; a program needn't handle non-finite values.
Results may differ from a plain program's by a relative error of at most 0.02.
Values may be sent and summed in bfloat16 or wider, within the bound.
A program may use at most 128 MiB of HBM per device.

v0:
```python
import jax
import jax.numpy as jnp
from jax import lax
from jax.sharding import PartitionSpec as P

DH = 128


def partner_2(value, axis, bit):
    return lax.ppermute(value, axis, [(i, i ^ 1 << bit) for i in range(lax.axis_size(axis))])


def body(queries, keys, values, residual, event_ids, lengths, type_weight, w_out, gain):
    seq = queries.shape[2]
    heads_width = queries.shape[3]
    width = residual.shape[3]
    head_size = DH
    heads = heads_width // head_size
    own = lax.axis_index(("dp", "fsdp"))
    length = lengths[own]
    count = jnp.sum(lengths).astype(jnp.float32)
    my_gain = gain[0]
    full_weight = lax.all_gather(w_out[0], "fsdp", axis=0, tiled=True)
    arrange = lambda matrix: matrix
    restore = lambda matrix: matrix
    query_heads = queries[0, 0].reshape(seq, heads, head_size)
    key_heads = keys[0, 0].reshape(seq, heads, head_size)
    value_heads = values[0, 0].reshape(seq, heads, head_size)
    scale = jnp.sqrt(jnp.float32(head_size))
    scores = (
        jnp.einsum("qhd,khd->hqk", query_heads, key_heads, preferred_element_type=jnp.float32)
        / scale
    )
    rows = jnp.arange(seq, dtype=jnp.int32)[:, None]
    cols = jnp.arange(seq, dtype=jnp.int32)[None, :]
    valid = (cols <= rows) & (cols < length)
    scores = jnp.where(valid[None], scores, jnp.float32(-1e30))
    probs = jax.nn.softmax(scores, axis=-1)
    probs_b = probs.astype(jnp.bfloat16)
    attn = (
        jnp.einsum("hqk,khd->qhd", probs_b, value_heads, preferred_element_type=jnp.float32)
        .reshape(seq, heads_width)
        .astype(jnp.bfloat16)
    )
    hidden = residual[0, 0].astype(jnp.float32) + jnp.dot(
        arrange(attn), full_weight, preferred_element_type=jnp.float32
    )
    inv = lax.rsqrt(jnp.mean(hidden * hidden, axis=-1, keepdims=True) + 1e-06)
    normed = hidden * inv
    feat = normed * my_gain[None, :]
    partner = partner_2(feat.astype(jnp.bfloat16), "copy", 0)
    type_count = type_weight.shape[0]
    matches = event_ids[0][:, None] == jnp.arange(type_count, dtype=jnp.int32)[None, :]
    looked_up = jnp.sum(jnp.where(matches, type_weight[None, :], jnp.float32(0.0)), axis=-1)
    live = jnp.arange(seq, dtype=jnp.int32) < length
    tok_w = jnp.where(live, looked_up, jnp.float32(0.0))
    diff = feat - partner.astype(jnp.float32)
    loss = jnp.sum(tok_w * jnp.sum(diff * diff, axis=-1)) / (width * count)
    dfeat = 2.0 * tok_w[:, None] * diff / (width * count)
    scaled = dfeat * my_gain[None, :]
    d_hidden = (inv * (scaled - normed * jnp.mean(normed * scaled, axis=-1, keepdims=True))).astype(
        jnp.bfloat16
    )
    partial_term = jnp.dot(attn.T, d_hidden, preferred_element_type=jnp.float32).astype(
        jnp.bfloat16
    )
    row_sum = lax.psum_scatter(partial_term, "fsdp", scatter_dimension=0, tiled=True).astype(
        jnp.float32
    )
    d_wo = lax.psum(row_sum.astype(jnp.bfloat16), "dp").astype(jnp.float32)
    d_attn_arranged = lax.dot_general(
        d_hidden, full_weight, (((1,), (1,)), ((), ())), preferred_element_type=jnp.float32
    )
    d_attn = restore(d_attn_arranged).astype(jnp.bfloat16)
    d_heads = d_attn.reshape(seq, heads, head_size)
    d_values = (
        jnp.einsum("hqk,qhd->khd", probs_b, d_heads, preferred_element_type=jnp.float32)
        .reshape(seq, heads_width)
        .astype(jnp.bfloat16)
    )
    dprob = jnp.einsum("qhd,khd->hqk", d_heads, value_heads, preferred_element_type=jnp.float32)
    delta = jnp.sum(dprob * probs, axis=-1, keepdims=True)
    ds = (probs * (dprob - delta) / scale).astype(jnp.bfloat16)
    d_queries = (
        jnp.einsum("hqk,khd->qhd", ds, key_heads, preferred_element_type=jnp.float32)
        .reshape(seq, heads_width)
        .astype(jnp.bfloat16)
    )
    d_keys = (
        jnp.einsum("hqk,qhd->khd", ds, query_heads, preferred_element_type=jnp.float32)
        .reshape(seq, heads_width)
        .astype(jnp.bfloat16)
    )
    return (
        loss.reshape(1, 1),
        d_queries[None, None],
        d_keys[None, None],
        d_values[None, None],
        d_wo[None],
    )


def solution(mesh):
    in_specs = (
        P("copy", ("dp", "fsdp"), None, None),
        P("copy", ("dp", "fsdp"), None, None),
        P("copy", ("dp", "fsdp"), None, None),
        P("copy", ("dp", "fsdp"), None, None),
        P(("dp", "fsdp"), None),
        P(),
        P(),
        P("copy", "fsdp", None),
        P("copy", None),
    )
    out_specs = (
        P("copy", ("dp", "fsdp")),
        P("copy", ("dp", "fsdp"), None, None),
        P("copy", ("dp", "fsdp"), None, None),
        P("copy", ("dp", "fsdp"), None, None),
        P("copy", "fsdp", None),
    )
    return jax.shard_map(body, mesh=mesh, in_specs=in_specs, out_specs=out_specs, check_vma=False)
```

profile of v0, /device:TPU:1, one launch (start us, length us, event | category | flops | bytes accessed | tf_op | source)
XLA Modules:
  0.0 437.5 jit_solution(15980191786920070180)
XLA Ops:
  7.2 0.0 copy-start.3
  7.2 0.0 all-gather.3.cloned.1.call-start
  7.2 0.7 all-gather.3.cloned.1.call-update
  7.9 0.0 reduce-scatter.2.cloned.1.call-start
  8.0 1.6 copy.48
  9.6 0.0 copy-start
  9.6 0.0 copy-done.3
  9.6 0.0 copy-start.9
  9.6 0.0 copy-start.6
  9.6 1.4 copy.44
  11.1 0.0 copy-start.4
  11.1 2.5 copy.45
  13.6 0.0 copy-done.9
  13.6 0.6 dynamic_slice.3
  14.2 0.0 copy-done.6
  14.2 0.7 iota_compare_fusion.2
  14.9 0.1 fusion.35
  15.0 0.0 copy-done.4
  15.0 5.6 %fusion.44 = (f32[20,256]{1,0:T(8,128)S(1)}, f32[20,256,256]{1,2,0:T(8,128)}) fusion(pred[256,256]{0,1:T(8,128)(4,1)S(1)} %fusion.35, bf16[256,20,128]{0,2,1:T(8,128)(2,1)S(1)} %bitcast.52, bf16[256,20,128]{0,2,1:T(8,128)(2,1)} %bitcast.54), kind=kOutput, calls=%fused_computation.52 | convolution fusion | flops 340787456 | bytes 7950336 | tf_op jit(solution)/shard_map/sub | solution.py:38
  20.6 0.0 copy-done
  20.6 4.1 convolution_convert_fusion.1
  24.7 137.1 %all-gather.3.cloned.1.call-done = bf16[1,2560,2560]{2,1,0:T(8,128)(2,1)} async-done(((bf16[1,160,2560]{2,1,0:T(8,128)(2,1)}), bf16[1,2560,2560]{2,1,0:T(8,128)(2,1)}) %all-gather.3.cloned.1.call-update) | async-done | bytes 13107216 | tf_op jit(solution)/shard_map/all_gather | solution.py:23
  161.8 9.2 %multiply_reduce_fusion.3 = (f32[256]{0:T(256)S(1)}, f32[256,2560]{1,0:T(8,128)S(1)}) fusion(bf16[256,2560]{0,1:T(8,128)(2,1)} %bitcast.50, bf16[1,2560,2560]{2,1,0:T(8,128)(2,1)} %all-gather.3.cloned.1.call-done, bf16[1,1,256,2560]{3,2,1,0:T(8,128)(2,1)} %param.12), kind=kOutput, calls=%fused_computation.22 | convolution fusion | flops 3358064384 | bytes 18351104 | tf_op jit(solution)/shard_map/dot_general | solution.py:45
  170.9 0.0 copy-start.7
  170.9 0.0 copy-start.8
  171.0 1.3 multiply_convert_fusion.2
  172.3 2.4 collective-permute-start
  174.8 0.7 reduce_sum.77
  176.0 0.0 copy-start.2
  176.0 0.0 copy-done.7
  176.1 0.0 copy-done.8
  176.1 0.2 select_reduce_fusion
  176.3 0.8 select_multiply_fusion
  177.1 26.5 %collective-permute-done = bf16[256,2560]{1,0:T(8,128)(2,1)} collective-permute-done((bf16[256,2560]{1,0:T(8,128)(2,1)}, bf16[256,2560]{1,0:T(8,128)(2,1)}, u32[]{:S(2)}, u32[]{:S(2)}) %collective-permute-start) | collective-permute-done | bytes 1310752 | tf_op jit(solution)/shard_map/ppermute | solution.py:10
  203.6 2.4 multiply_reduce_fusion.1
  206.1 0.0 copy-done.2
  206.1 8.6 %convolution_convert_fusion = bf16[2560,2560]{1,0:T(8,128)(2,1)} fusion(bf16[256,2560]{0,1:T(8,128)(2,1)S(1)} %bitcast.51, f32[256,2560]{1,0:T(8,128)S(1)} %get-tuple-element.25, bf16[256,2560]{1,0:T(8,128)(2,1)} %collective-permute-done, f32[256]{0:T(256)S(1)} %broadcast_multiply_fusion, f32[]{:T(128)S(6)} %mul.91, f32[256]{0:T(256)S(1)} %select_multiply_fusion, ...), kind=kOutput, calls=%fused_computation.2 | convolution fusion | flops 3369205760 | bytes 18363396 | tf_op jit(solution)/shard_map/dot_general | solution.py:64
  214.7 0.0 reduce-scatter.2.cloned.1.call-update
  214.7 0.2 all-reduce.2.cloned.1.call-start
  215.0 1.2 multiply_reduce_fusion.4
  216.9 10.0 %fusion.11 = bf16[256,2560]{1,0:T(8,128)(2,1)} fusion(bf16[1,2560,2560]{2,1,0:T(8,128)(2,1)} %all-gather.3.cloned.1.call-done, f32[256,2560]{1,0:T(8,128)S(1)} %get-tuple-element.25, bf16[256,2560]{1,0:T(8,128)(2,1)} %collective-permute-done, f32[256]{0:T(256)S(1)} %broadcast_multiply_fusion, f32[]{:T(128)S(6)} %mul.91, f32[256]{0:T(256)S(1)} %select_multiply_fusion, ...), kind=kOutput, calls=%fused_computation.14 | convolution fusion | flops 3363307520 | bytes 18363396 | tf_op jit(solution)/shard_map/dot_general | solution.py:71
  226.9 0.0 copy-start.1
  226.9 1.7 copy.50
  228.6 0.0 copy-done.1
  228.6 3.2 fusion.45
  231.8 10.4 %fusion.27 = bf16[20,256,128]{1,2,0:T(8,128)(2,1)} fusion(bf16[256,20,128]{0,2,1:T(8,128)(2,1)} %bitcast.55, f32[20,256,256]{1,2,0:T(8,128)} %fusion.45, f32[20,256,256]{1,2,0:T(8,128)} %get-tuple-element.23, f32[20,256]{1,0:T(8,128)S(1)} %get-tuple-element.22), kind=kOutput, calls=%fused_computation.30 | convolution fusion | flops 345380096 | bytes 13127680 | tf_op jit(solution)/shard_map/hqk,khd->qhd/dot_general | solution.py:85
  242.2 0.0 copy-start.5
  242.2 2.5 copy.56
  244.7 0.0 copy-done.5
  244.7 10.1 %fusion.30 = bf16[20,256,128]{1,2,0:T(8,128)(2,1)} fusion(bf16[256,20,128]{0,2,1:T(8,128)(2,1)S(1)} %bitcast.53, f32[20,256,256]{1,2,0:T(8,128)} %fusion.45, f32[20,256,256]{1,2,0:T(8,128)} %get-tuple-element.23, f32[20,256]{1,0:T(8,128)S(1)} %get-tuple-element.22), kind=kOutput, calls=%fused_computation.31 | convolution fusion | flops 345380096 | bytes 13127680 | tf_op jit(solution)/shard_map/hqk,qhd->khd/dot_general | solution.py:90
  254.8 2.4 copy.57
  257.3 105.0 %reduce-scatter.2.cloned.1.call-done = bf16[160,2560]{1,0:T(8,128)(2,1)} async-done(((bf16[2560,2560]{1,0:T(8,128)(2,1)}), bf16[160,2560]{1,0:T(8,128)(2,1)}) %reduce-scatter.2.cloned.1.call-update) | async-done | bytes 819216 | tf_op jit(solution)/shard_map/reduce_scatter | solution.py:67
  362.3 0.0 all-reduce.2.cloned.1.call-update
  362.3 3.5 convolution_convert_fusion.2
  365.8 1.6 copy.58
  367.4 59.9 %all-reduce.2.cloned.1.call-done = bf16[1,160,2560]{2,1,0:T(8,128)(2,1)} async-done(((bf16[1,160,2560]{2,1,0:T(8,128)(2,1)}), bf16[1,160,2560]{2,1,0:T(8,128)(2,1)}) %all-reduce.2.cloned.1.call-update) | async-done | bytes 819216 | tf_op jit(solution)/shard_map/psum | solution.py:70
  427.3 2.5 broadcast_in_dim.54
  (3 shorter events, 0.0 us)
Async XLA Ops:
  7.2 2.4 copy-start.3
  7.2 154.6 %all-gather.3.cloned.1.call-start = ((), (), s32[]{:S(2)}) async-start(), calls=%async_computation.3 | async-start | bytes 13926400 | tf_op jit(solution)/shard_map/all_gather | solution.py:23
  7.9 354.4 %reduce-scatter.2.cloned.1.call-start = ((), (), s32[]{:S(2)}) async-start(), calls=%async_computation.1 | async-start | bytes 13926400 | tf_op jit(solution)/shard_map/reduce_scatter | solution.py:67
  9.6 11.0 %copy-start = (bf16[1,1,256,2560]{2,3,1,0:T(8,128)(2,1)}, bf16[1,1,256,2560]{2,3,1,0:T(8,128)(2,1)S(1)}, u32[]{:S(2)}) copy-start(bf16[1,1,256,2560]{2,3,1,0:T(8,128)(2,1)S(1)} %copy.48) | copy-start | bytes 3932164
  9.6 4.0 copy-start.9
  9.6 4.6 %copy-start.6 = (f32[1,2560]{1,0:T(1,128)S(1)}, f32[1,2560]{1,0:T(1,128)}, u32[]{:S(2)}) copy-start(f32[1,2560]{1,0:T(1,128)} %param.17) | copy-start | bytes 30724
  11.1 3.9 copy-start.4
  170.9 5.1 %copy-start.7 = (f32[1024]{0:T(1024)S(1)}, f32[1024]{0:T(1024)}, u32[]{:S(2)}) copy-start(f32[1024]{0:T(1024)} %param.15) | copy-start | bytes 12292
  170.9 5.1 %copy-start.8 = (s32[1,256]{1,0:T(1,128)S(1)}, s32[1,256]{1,0:T(1,128)}, u32[]{:S(2)}) copy-start(s32[1,256]{1,0:T(1,128)} %param.13) | copy-start | bytes 3076
  172.3 31.3 %collective-permute-start = (bf16[256,2560]{1,0:T(8,128)(2,1)}, bf16[256,2560]{1,0:T(8,128)(2,1)}, u32[]{:S(2)}, u32[]{:S(2)}) collective-permute-start(bf16[256,2560]{1,0:T(8,128)(2,1)} %multiply_convert_fusion.2), channel_id=1, source_target_pairs={{0,128},{128,0},{1,129},{129,1},{2,130},{130,2},{3,131},{131,3},{4... | collective-permute-start | bytes 3932168 | tf_op jit(solution)/shard_map/ppermute | solution.py:10
  176.0 30.1 %copy-start.2 = (bf16[20,256,128]{1,2,0:T(8,128)(2,1)S(1)}, bf16[20,256,128]{1,2,0:T(8,128)(2,1)}, u32[]{:S(2)}) copy-start(bf16[20,256,128]{1,2,0:T(8,128)(2,1)} %convolution_convert_fusion.1) | copy-start | bytes 3932164
  214.7 212.6 %all-reduce.2.cloned.1.call-start = ((), (), s32[]{:S(2)}) async-start(), calls=%async_computation.2 | async-start | bytes 1638400 | tf_op jit(solution)/shard_map/psum | solution.py:70
  226.9 1.7 copy-start.1
  242.2 2.5 copy-start.5
Sparse Core Ops, SparseCore 0:
  9.8 151.9 all-gather.2
  214.9 147.3 reduce-scatter.1
  364.7 62.6 all-reduce.1
where the time goes:
time: 439 us; the launch traced here: 437 us
  waiting for transfers between devices  329 us (75%)
  matrix products  64.7 us (15%)
  between operations  16.3 us (4%)
  local copies, waits for them, and re-layouts  14.4 us (3%)
  other arithmetic  9.98 us (2%)
    all_gather x1, waiting for transfers between devices, body(): full_weight = lax.all_gather(w_out[0], 'fsdp', axis=0, tiled=True)  137 us
    reduce_scatter x1, waiting for transfers between devices, body(): lax.psum_scatter(partial_term, 'fsdp', scatter_dimension=0, tiled=True)  105 us
    psum x1, waiting for transfers between devices, body(): d_wo = lax.psum(row_sum.astype(jnp.bfloat16), 'dp').astype(jnp.float32)  59.9 us
    ppermute x1, waiting for transfers between devices, partner_2(): lax.ppermute(value, axis, [(i, i ^ 1 << bit) for i in range(lax.axis_size...  26.5 us
    unnamed x26, local copies, waits for them, and re-layouts  12.1 us
    dot_general x1, matrix products, body(): jnp.einsum('hqk,khd->qhd', ds, key_heads, preferred_element_type=jnp.floa...  10.4 us
    dot_general x1, matrix products, body(): jnp.einsum('hqk,qhd->khd', ds, query_heads, preferred_element_type=jnp.fl...  10.1 us
    dot_general x1, matrix products, body(): lax.dot_general(d_hidden, full_weight, (((1,), (1,)), ((), ())), preferre...  10 us
  transfers between devices with their start and end apart: 4, of which 4 were waited for; matrix products, arithmetic and copies ran while one was open for 15% of the time, Pallas kernels for 0%

commit v1 on v0

v1 whole, which is shorter than its diff:
```python
import jax
import jax.numpy as jnp
from jax import lax
from jax.experimental import pallas as pl
from jax.experimental.pallas import tpu as pltpu
from jax.sharding import PartitionSpec as P

MESH = pl.DeviceIdType.MESH
F32 = jnp.float32
BF16 = jnp.bfloat16
L, D, H, DH = 256, 2560, 20, 128
BLK = 160
HALF = 80
QW = 640
CW = 1280
AW, BW = 256, 384
SCALE = 128.0**0.5
NT = (((1,), (1,)), ((), ()))
TN = (((0,), (0,)), ((), ()))
NEAR = (0, -1, 1, -2, 2, -3, 3, -4)


def dot(a, b, dims=(((1,), (0,)), ((), ()))):
    return lax.dot_general(a, b, dims, preferred_element_type=F32)


def kernel(
    q_ref, k_ref, v_ref, res_ref, w_ref, ids_ref, len_ref, tw_ref, gain_ref,
    loss_ref, dq_ref, dk_ref, dv_ref, dwo_ref,
    wf, at, hid, pb, gp, dh, dhs, probs, bias, pbuf, za, zaf, xa, xb, zb, fsum, yrx, rows,
    s_send, s_zr, s_xr, s_yr, s_sib, s_pr, s_misc, s_za, s_xa, s_xb, s_zb, s_fin,
):
    attn, hb = dk_ref, dq_ref
    c = lax.axis_index("copy")
    d = lax.axis_index("dp")
    f = lax.axis_index("fsdp")
    x, core = d // 2, d % 2
    y, z = f // 8, f % 8
    own = d * 16 + f

    def at_z(step):
        return (c, d, y * 8 + (z + step + 8) % 8)

    def at_x(step):
        return (c, ((x + step + 4) % 4) * 2 + core, f)

    other_y = (c, d, (1 - y) * 8 + z)
    sibling = (c, x * 2 + 1 - core, f)
    partner = (1 - c, d, f)

    def send(src, dst, group, recv, device):
        copy = pltpu.make_async_remote_copy(
            src_ref=src, dst_ref=dst, send_sem=s_send.at[group], recv_sem=recv,
            device_id=device, device_id_type=MESH,
        )
        copy.start()

    def arrived(ref, sem):
        pltpu.make_async_copy(ref, ref, sem).wait()

    barrier = pltpu.get_barrier_semaphore()
    greet = (at_z(1), at_z(-1), at_x(1), at_x(-1), at_x(2), other_y, sibling, partner)
    for device in greet:
        pl.semaphore_signal(barrier, inc=1, device_id=device, device_id_type=MESH)
    pl.semaphore_wait(barrier, len(greet))

    def piece(yy, zz, quarter):
        row = pl.multiple_of((yy * 8 + (zz + 16) % 8) * BLK + core * HALF, 16)
        col = pl.multiple_of(((quarter + 8) % 4) * QW, 128)
        return wf.at[pl.ds(row, HALF), pl.ds(col, QW)]

    def own_piece(quarter):
        col = pl.multiple_of(((quarter + 8) % 4) * QW, 128)
        return w_ref.at[pl.ds(pl.multiple_of(core * HALF, 16), HALF), pl.ds(col, QW)]

    ORDER = (0, 1, -1, 2)

    def steps(s, way):
        return 4 if (s + way) % 2 == 0 else 3

    def z_where(s):
        return ((1 - y), x) if s == 0 else (y, x + ORDER[s - 1])

    def to_sibling(ref, i):
        send(ref, ref, 0, s_sib.at[i], sibling)

    def z_event(s, k):
        yy, quarter = z_where(s)
        i = 0 if s == 0 else s - 1
        for way, sign in ((0, 1), (1, -1)):
            last = steps(s, way)
            if 0 < k <= last:
                got = piece(yy, z - sign * k, quarter)
                arrived(got, s_zr.at[s, way, k - 1])
                if k < last:
                    send(got, got, 0, s_zr.at[s, way, k], at_z(sign))
                if s == 0:
                    x_send(NEAR.index(-sign * k) if k < 4 else 7)
                to_sibling(got, i)
            elif k == 0:
                dst = piece(yy, z, quarter)
                src = dst if s == 0 else own_piece(quarter)
                send(src, dst, 0, s_zr.at[s, way, 0], at_z(sign))

    def x_send(m):
        got = piece(1 - y, z + NEAR[m], x)
        send(got, got, 0, s_xr.at[0, m], at_x(1))
        send(got, got, 0, s_xr.at[1, m], at_x(-1))

    def x_event(m):
        for way, sign in ((0, 1), (1, -1)):
            got = piece(1 - y, z + NEAR[m], x - sign)
            arrived(got, s_xr.at[way, m])
            if m % 2 == way:
                send(got, got, 0, s_xr.at[way, 8 + m // 2], at_x(sign))
            to_sibling(got, 1 if way == 1 else 2)

    def x_last(n):
        for way in (0, 1):
            got = piece(1 - y, z + NEAR[2 * n + way], x + 2)
            arrived(got, s_xr.at[way, 8 + n])
            to_sibling(got, 3)

    src = own_piece(x)
    send(src, piece(y, z, x), 0, s_yr.at[0], other_y)
    z_event(1, 0)
    z_event(2, 0)
    send(gain_ref, gp, 1, s_misc.at[0], partner)
    local = pltpu.make_async_copy(
        w_ref, wf.at[pl.ds(pl.multiple_of(f * BLK, 16), BLK), :], s_misc.at[2]
    )
    local.start()

    lane = lax.broadcasted_iota(jnp.int32, (1, 128), 1)
    lens = len_ref[...]
    count = jnp.sum(lens).astype(F32)
    length = jnp.sum(jnp.where(lane == own, lens, 0), axis=-1, keepdims=True)
    r_at = lax.broadcasted_iota(jnp.int32, (L, L), 0)
    c_at = lax.broadcasted_iota(jnp.int32, (L, L), 1)
    bias[...] = jnp.where((c_at <= r_at) & (c_at < length), F32(0.0), F32(-1e30))

    def head(h):
        return pl.ds(pl.multiple_of(h * DH, DH), DH)

    def forward(h, carry):
        cols = head(h)
        s = dot(q_ref[:, cols], k_ref[:, cols], NT) * F32(1.0 / SCALE) + bias[...]
        e = jnp.exp(s - jnp.max(s, axis=-1, keepdims=True))
        p = (e / jnp.sum(e, axis=-1, keepdims=True)).astype(BF16)
        probs[h] = p
        a = dot(p, v_ref[:, cols])
        attn[:, cols] = a.astype(BF16)
        at[cols, 0:L] = a.T.astype(BF16)
        return carry

    def heads(first, n):
        lax.fori_loop(first, first + n, forward, 0)

    heads(0, 2)
    got = piece(1 - y, z, x)
    arrived(got, s_yr.at[0])
    z_event(0, 0)
    x_send(0)
    to_sibling(got, 0)
    heads(2, 3)
    z_event(1, 1)
    z_event(0, 1)
    heads(5, 3)
    z_event(1, 2)
    z_event(0, 2)
    x_event(0)
    heads(8, 4)
    z_event(1, 3)
    z_event(0, 3)
    x_event(1)
    x_event(2)
    heads(12, 4)
    z_event(1, 4)
    z_event(0, 4)
    z_event(2, 1)
    z_event(3, 0)
    x_event(3)
    x_event(4)
    heads(16, 4)
    send(at.at[:, 0:L], at.at[:, L : 2 * L], 1, s_misc.at[1], sibling)
    z_event(2, 2)
    z_event(3, 1)
    z_event(4, 0)
    x_event(5)
    x_event(6)

    type_at = lax.broadcasted_iota(jnp.int32, (1, 1024), 1)
    looked = jnp.sum(
        jnp.where(ids_ref[...] == type_at, tw_ref[...], F32(0.0)), axis=-1, keepdims=True
    )
    live = lax.broadcasted_iota(jnp.int32, (L, 1), 0) < length
    rows[:, 0:1] = jnp.where(live, looked, F32(0.0))
    rows[:, 1:2] = jnp.zeros((L, 1), F32)
    rows[:, 2:3] = jnp.zeros((L, 1), F32)
    local.wait()

    def quarter_cols(i):
        return pl.ds(pl.multiple_of(((x + ORDER[i] + 4) % 4) * QW, 128), QW)

    def hidden(i):
        arrived(wf.at[0 : 15 * HALF, 0:QW], s_sib.at[i])
        cols = quarter_cols(i)
        hc = res_ref[:, cols].astype(F32) + dot(attn[...], wf[:, cols])
        hid[:, cols] = hc
        hb[:, cols] = hc.astype(BF16)
        rows[:, 1:2] += jnp.sum(hc * hc, axis=-1, keepdims=True)
        send(hb.at[:, cols], pb.at[:, cols], 2, s_pr.at[i], partner)

    def partner_square(i):
        cols = quarter_cols(i)
        arrived(pb.at[:, cols], s_pr.at[i])
        part = pb[:, cols].astype(F32)
        rows[:, 2:3] += jnp.sum(part * part, axis=-1, keepdims=True)

    hidden(0)
    z_event(2, 3)
    z_event(3, 2)
    z_event(4, 1)
    x_event(7)
    z_event(2, 4)
    hidden(1)
    z_event(3, 3)
    z_event(4, 2)
    for n in range(4):
        x_last(n)
    z_event(3, 4)
    hidden(2)
    z_event(4, 3)
    z_event(4, 4)
    hidden(3)
    arrived(gp, s_misc.at[0])
    arrived(at.at[:, L : 2 * L], s_misc.at[1])
    for i in range(4):
        partner_square(i)

    tok = rows[:, 0:1]
    inv = lax.rsqrt(rows[:, 1:2] * F32(1.0 / D) + F32(1e-06))
    inv_p = lax.rsqrt(rows[:, 2:3] * F32(1.0 / D) + F32(1e-06))
    coef = 2.0 * tok / (D * count)
    rows[:, 3:4] = jnp.zeros((L, 1), F32)
    rows[:, 4:5] = jnp.zeros((L, 1), F32)

    def chunk(t):
        return pl.ds(pl.multiple_of(t * 256, 256), 256)

    def stats(t, carry):
        cols = chunk(t)
        n = hid[:, cols] * inv
        g = gain_ref[:, cols]
        diff = n * g - pb[:, cols].astype(F32) * inv_p * gp[:, cols]
        scaled = diff * g
        rows[:, 3:4] += jnp.sum(diff * diff, axis=-1, keepdims=True)
        rows[:, 4:5] += jnp.sum(n * scaled, axis=-1, keepdims=True)
        return carry

    lax.fori_loop(0, 10, stats, 0)
    loss_ref[...] = jnp.sum(tok * rows[:, 3:4], axis=0, keepdims=True) / (D * count)
    mean = rows[:, 4:5] * F32(1.0 / D)

    def grads(t, carry):
        cols = chunk(t)
        n = hid[:, cols] * inv
        g = gain_ref[:, cols]
        diff = n * g - pb[:, cols].astype(F32) * inv_p * gp[:, cols]
        dh[:, cols] = (inv * coef * (diff * g - n * mean)).astype(BF16)
        return carry

    lax.fori_loop(0, 10, grads, 0)
    other_half = pl.ds(pl.multiple_of((1 - core) * CW, 128), CW)
    send(dh.at[:, other_half], dhs, 1, s_misc.at[3], sibling)
    arrived(dhs, s_misc.at[3])

    def term(row, n_rows, col, width):
        r = pl.ds(pl.multiple_of(row, 16), n_rows)
        mine = dh[:, pl.ds(pl.multiple_of(core * CW + col, 128), width)]
        return dot(at[r, 0:L], mine) + dot(at[r, L : 2 * L], dhs[:, col : col + width])

    def block_row(yy, zz):
        return (yy * 8 + (zz + 16) % 8) * BLK

    WAYS = ((0, 1), (1, -1))

    def b_first(t):
        for way, sign in WAYS:
            for yy in (0, 1):
                val = term(block_row(yy, z - sign * (1 + t)), BLK, 2 * AW + way * BW, BW)
                pbuf[way, t, :, yy] = val.reshape(4, 40, BW).astype(BF16)
            send(
                pbuf.at[way, t, (x - sign + 4) % 4], xb.at[way, 0, t], 4,
                s_xb.at[way, 0, t], at_x(sign),
            )

    def b_next(t, k):
        for way, sign in WAYS:
            slot = xb.at[way, k - 1, t]
            arrived(slot, s_xb.at[way, k - 1, t])
            mine = pbuf[way, t, (x - sign * (1 + k) + 8) % 4]
            slot[...] = (slot[...].astype(F32) + mine.astype(F32)).astype(BF16)
            send(slot, xb.at[way, k, t], 4, s_xb.at[way, k, t], at_x(sign))

    def b_sum(way, t):
        slot = xb.at[way, 2, t]
        arrived(slot, s_xb.at[way, 2, t])
        return slot[...].astype(F32) + pbuf[way, t, x].astype(F32)

    def b_z(t):
        for way, sign in WAYS:
            val = b_sum(way, t)
            slot = zb.at[way, t]

            @pl.when(t == 0)
            def _():
                slot[...] = val.astype(BF16)

            @pl.when(t > 0)
            def _():
                arrived(slot, s_zb.at[way, t])
                slot[...] = (slot[...].astype(F32) + val).astype(BF16)

            send(slot, zb.at[way, t + 1], 5, s_zb.at[way, t + 1], at_z(sign))

    def a_step(t):
        for yy in (0, 1):
            for way, sign in WAYS:
                val = term(block_row(yy, z - sign * (1 + t)), BLK, way * AW, AW)
                slot = za.at[way, yy, t]

                @pl.when(t == 0)
                def _():
                    slot[...] = val.astype(BF16)

                @pl.when(t > 0)
                def _():
                    arrived(slot, s_za.at[way, yy, t])
                    slot[...] = (slot[...].astype(F32) + val).astype(BF16)

                send(slot, za.at[way, yy, t + 1], 3, s_za.at[way, yy, t + 1], at_z(sign))

    def a_last():
        for way, sign in WAYS:
            for yy in (0, 1):
                slot = za.at[way, yy, 7]
                arrived(slot, s_za.at[way, yy, 7])
                val = slot[...].astype(F32) + term(block_row(yy, z), BLK, way * AW, AW)
                zaf[way, :, yy] = val.reshape(4, 40, AW).astype(BF16)
            send(zaf.at[way, (x - sign + 4) % 4], xa.at[way, 0], 6, s_xa.at[way, 0], at_x(sign))

    def a_next(k):
        for way, sign in WAYS:
            slot = xa.at[way, k - 1]
            arrived(slot, s_xa.at[way, k - 1])
            mine = zaf[way, (x - sign * (1 + k) + 8) % 4]
            slot[...] = (slot[...].astype(F32) + mine.astype(F32)).astype(BF16)
            send(slot, xa.at[way, k], 6, s_xa.at[way, k], at_x(sign))

    def pair(t):
        cols2 = pl.ds(pl.multiple_of(t * 256, 256), 256)
        da2 = dot(dh[...], wf[cols2, :], NT).astype(BF16)
        for j in (0, 1):
            cols = pl.ds(pl.multiple_of(t * 256 + j * DH, DH), DH)
            da = da2[:, j * DH : (j + 1) * DH]
            p = probs[2 * t + j]
            dv_ref[:, cols] = dot(p, da, TN).astype(BF16)
            dprob = dot(da, v_ref[:, cols], NT)
            pf = p.astype(F32)
            delta = jnp.sum(dprob * pf, axis=-1, keepdims=True)
            ds = (pf * (dprob - delta) * F32(1.0 / SCALE)).astype(BF16)
            dq_ref[:, cols] = dot(ds, k_ref[:, cols]).astype(BF16)
            dk_ref[:, cols] = dot(ds, q_ref[:, cols], TN).astype(BF16)

    arrived(pb, s_send.at[2])

    def tick(t, carry):
        @pl.when(t < 8)
        def _():
            b_first(t)

        @pl.when(t < 7)
        def _():
            a_step(t)

        @pl.when((t >= 1) & (t < 9))
        def _():
            b_next(t - 1, 1)

        @pl.when((t >= 2) & (t < 10))
        def _():
            b_next(t - 2, 2)

        @pl.when((t >= 3) & (t < 10))
        def _():
            b_z(t - 3)

        @pl.when(t == 7)
        def _():
            a_last()

        @pl.when(t == 8)
        def _():
            a_next(1)

        @pl.when(t == 9)
        def _():
            a_next(2)

        pair(t)
        return carry

    lax.fori_loop(0, 10, tick, 0)

    for way, sign in WAYS:
        slot = xa.at[way, 2]
        arrived(slot, s_xa.at[way, 2])
        val = slot[...].astype(F32) + zaf[way, x].astype(F32)
        fsum[:, :, way * AW : (way + 1) * AW] = val.astype(BF16)
    for way, sign in WAYS:
        val = b_sum(way, 7)
        slot = zb.at[way, 7]
        arrived(slot, s_zb.at[way, 7])
        lo = 2 * AW + way * BW
        fsum[:, :, lo : lo + BW] = (slot[...].astype(F32) + val).astype(BF16)
    send(fsum.at[1 - y], yrx, 7, s_fin.at[0], other_y)
    half = pl.ds(pl.multiple_of(core * CW, 128), CW)
    arrived(yrx, s_fin.at[0])
    dwo_ref[x, :, half] = (yrx[...].astype(F32) + fsum[y].astype(F32)).astype(BF16)
    mine = dwo_ref.at[x, :, half]
    for i, step in enumerate((1, -1, 2)):
        send(mine, mine, 7, s_fin.at[1 + i], at_x(step))
    send(mine, mine, 7, s_fin.at[4], sibling)
    for i, step in enumerate((1, -1, 2)):
        got = dwo_ref.at[(x - step + 4) % 4, :, half]
        arrived(got, s_fin.at[1 + i])
        send(got, got, 7, s_fin.at[5 + i], sibling)
    for i, step in enumerate((0, 1, -1, 2)):
        got = dwo_ref.at[(x - step + 4) % 4, :, other_half]
        arrived(got, s_fin.at[4 + i])

    arrived(wf.at[0 : 32 * HALF, 0:QW], s_send.at[0])
    arrived(wf.at[0 : 32 * HALF, 0:QW], s_send.at[0])
    arrived(wf.at[0 : 32 * HALF, 0:QW], s_send.at[0])
    arrived(wf.at[0 : 24 * HALF, 0:QW], s_send.at[0])
    arrived(gp, s_send.at[1])
    arrived(at.at[:, 0:L], s_send.at[1])
    arrived(dhs, s_send.at[1])
    for way in (0, 1):
        for yy in (0, 1):
            arrived(za.at[way, yy, 1:8], s_send.at[3])
        arrived(xb.at[way], s_send.at[4])
        arrived(zb.at[way, 1:8], s_send.at[5])
        arrived(xa.at[way], s_send.at[6])
    arrived(yrx, s_send.at[7])
    for _ in range(7):
        arrived(yrx, s_send.at[7])


def body(queries, keys, values, residual, event_ids, lengths, type_weight, w_out, gain):
    vmem = pl.BlockSpec(memory_space=pltpu.VMEM)
    dma = pltpu.SemaphoreType.DMA
    big = jax.ShapeDtypeStruct((L, D), BF16)
    loss, dq, dk, dv, dwo = pl.pallas_call(
        kernel,
        out_shape=(
            jax.ShapeDtypeStruct((1, 1), F32), big, big, big,
            jax.ShapeDtypeStruct((4, 40, D), BF16),
        ),
        in_specs=[vmem] * 9,
        out_specs=(vmem,) * 5,
        scratch_shapes=[
            pltpu.VMEM((D, D), BF16),
            pltpu.VMEM((D, 2 * L), BF16),
            pltpu.VMEM((L, D), F32),
            pltpu.VMEM((L, D), BF16),
            pltpu.VMEM((1, D), F32),
            pltpu.VMEM((L, D), BF16),
            pltpu.VMEM((L, CW), BF16),
            pltpu.VMEM((H, L, L), BF16),
            pltpu.VMEM((L, L), F32),
            pltpu.VMEM((2, 8, 4, 2, 40, BW), BF16),
            pltpu.VMEM((2, 2, 8, BLK, AW), BF16),
            pltpu.VMEM((2, 4, 2, 40, AW), BF16),
            pltpu.VMEM((2, 3, 2, 40, AW), BF16),
            pltpu.VMEM((2, 3, 8, 2, 40, BW), BF16),
            pltpu.VMEM((2, 8, 2, 40, BW), BF16),
            pltpu.VMEM((2, 40, CW), BF16),
            pltpu.VMEM((40, CW), BF16),
            pltpu.VMEM((L, 128), F32),
            dma((8,)),
            dma((5, 2, 4)),
            dma((2, 12)),
            dma((1,)),
            dma((4,)),
            dma((4,)),
            dma((4,)),
            dma((2, 2, 8)),
            dma((2, 3)),
            dma((2, 3, 8)),
            dma((2, 8)),
            dma((8,)),
        ],
        compiler_params=pltpu.CompilerParams(
            collective_id=0, has_side_effects=True, vmem_limit_bytes=67043328
        ),
        name="step",
    )(
        queries[0, 0], keys[0, 0], values[0, 0], residual[0, 0], w_out[0],
        event_ids.reshape(L, 1), lengths.reshape(1, 128), type_weight.reshape(1, 1024), gain,
    )
    return (
        loss, dq[None, None], dk[None, None], dv[None, None],
        dwo.reshape(BLK, D).astype(F32)[None],
    )


def solution(mesh):
    hist = P("copy", ("dp", "fsdp"), None, None)
    return jax.shard_map(
        body,
        mesh=mesh,
        in_specs=(
            hist, hist, hist, hist, P(("dp", "fsdp"), None), P(), P(),
            P("copy", "fsdp", None), P("copy", None),
        ),
        out_specs=(
            P("copy", ("dp", "fsdp")), hist, hist, hist, P("copy", "fsdp", None),
        ),
        check_vma=False,
    )
```

time: 439 us -> 157 us (0.36)
  waiting for transfers between devices: 329 us -> 0 us
  Pallas kernels: 0 us -> 146 us
  matrix products: 64.7 us -> 0 us
  between operations: 16.3 us -> 2.44 us
  local copies, waits for them, and re-layouts: 14.4 us -> 6.1 us
  other arithmetic: 9.98 us -> 2.58 us
    pallas_call x0 -> x1, Pallas kernels: none -> 146 us  [body(): pl.pallas_call(kernel, out_shape=(jax.ShapeDtypeStruct((1, 1), F32), big,...]
    all_gather x1 -> x0, waiting for transfers between devices: 137 us -> none  [body(): full_weight = lax.all_gather(w_out[0], 'fsdp', axis=0, tiled=True)]
    reduce_scatter x1 -> x0, waiting for transfers between devices: 105 us -> none  [body(): lax.psum_scatter(partial_term, 'fsdp', scatter_dimension=0, tiled=True)]
    psum x1 -> x0, waiting for transfers between devices: 59.9 us -> none  [body(): d_wo = lax.psum(row_sum.astype(jnp.bfloat16), 'dp').astype(jnp.float32)]
    dot_general x8 -> x0, matrix products: 59.1 us -> none  [the longest x1 10.4 us: body(): jnp.einsum('hqk,khd->qhd', ds, key_heads, preferred_element_type=jnp.floa...]
    ppermute x1 -> x0, waiting for transfers between devices: 26.5 us -> none  [partner_2(): lax.ppermute(value, axis, [(i, i ^ 1 << bit) for i in range(lax.axis_size...]
    unnamed x26 -> x9, local copies, waits for them, and re-layouts: 12.1 us -> 4.63 us
    sub x1 -> x0, matrix products: 5.59 us -> none  [body(): probs = jax.nn.softmax(scores, axis=-1)]
  transfers between devices with their start and end apart: 4 -> 0, of which waited for: 4 -> 0; matrix products, arithmetic and copies ran while one was open for 15% -> 0% of each run, Pallas kernels for 0% -> 0%
where the time goes in v1:
time: 157 us
  Pallas kernels  146 us (93%)
  local copies, waits for them, and re-layouts  6.1 us (4%)
  other arithmetic  2.58 us (2%)
  between operations  2.44 us (2%)
    pallas_call x1, Pallas kernels, body(): pl.pallas_call(kernel, out_shape=(jax.ShapeDtypeStruct((1, 1), F32), big,...  146 us
    unnamed x9, local copies, waits for them, and re-layouts  4.63 us

profile of v1, /device:TPU:1, one launch (start us, length us, event | category | flops | bytes accessed | tf_op | source)
XLA Modules:
  0.0 157.0 jit_solution(1810620096456215639)
XLA Ops:
  0.6 1.5 copy.14.ids_ref
  2.1 145.9 %step.1 = (f32[1,1]{1,0:T(1,128)}, bf16[256,2560]{1,0:T(8,128)(2,1)}, bf16[256,2560]{1,0:T(8,128)(2,1)}, bf16[256,2560]{1,0:T(8,128)(2,1)}, bf16[4,40,2560]{2,1,0:T(8,128)(2,1)}) custom-call(bf16[256,2560]{1,0:T(8,128)(2,1)} %bitcast.18, bf16[256,2560]{1,0:T(8,128)(2,1)} %bitcast.19, bf16[256,2560]{1,0:T(8,128)(2,1)} %bitcast.20, ...), custom_call_target="tpu_custom_call" | custom-call | tf_op jit(solution)/shard_map/step/pallas_call | solution.py:465
  148.0 0.0 copy-start.2
  148.0 2.6 %bitcast_convert_fusion = f32[1,160,2560]{2,1,0:T(8,128)} fusion(bf16[1,160,2560]{2,1,0:T(8,128)(2,1)} %bitcast.22), kind=kLoop, calls=%fused_computation | loop fusion | flops 409600 | bytes 2457600 | tf_op jit(solution)/shard_map/convert_element_type | solution.py:515
  151.2 0.0 copy-done.2
  151.2 0.0 copy-start.1
  151.2 1.1 copy.20
  152.3 0.7 copy-done.1
  153.0 0.0 copy-start
  153.0 1.1 copy.21
  154.1 0.7 copy-done
  154.8 1.1 copy.22
Async XLA Ops:
  148.0 3.2 %copy-start.2 = (bf16[256,2560]{1,0:T(8,128)(2,1)S(1)}, bf16[256,2560]{1,0:T(8,128)(2,1)}, u32[]{:S(2)}) copy-start(bf16[256,2560]{1,0:T(8,128)(2,1)} %get-tuple-element.11) | copy-start | bytes 3932164
  151.2 1.8 %copy-start.1 = (bf16[256,2560]{1,0:T(8,128)(2,1)S(1)}, bf16[256,2560]{1,0:T(8,128)(2,1)}, u32[]{:S(2)}) copy-start(bf16[256,2560]{1,0:T(8,128)(2,1)} %get-tuple-element.12) | copy-start | bytes 3932164
  153.0 1.8 %copy-start = (bf16[256,2560]{1,0:T(8,128)(2,1)S(1)}, bf16[256,2560]{1,0:T(8,128)(2,1)}, u32[]{:S(2)}) copy-start(bf16[256,2560]{1,0:T(8,128)(2,1)} %get-tuple-element.13) | copy-start | bytes 3932164
